TPU v7x, 512 devices: a whole 4x8x8 slice. The times are simulated.
512 devices in a mesh: row: 16 (over z, y_lo), col: 8 (over y_hi, core), rep: 4 (over x).
Axes of the slice: x: 4, y: 8 (y_hi: 4, y_lo: 2; y = y_hi * 2 + y_lo), z: 8, core: 2. Of those that a mesh axis runs over, the one named last changes fastest.
Arguments:
- genotypes: bfloat16 [2048, 16384], P(('row', 'col', 'rep')), may hold values from 0 to 2, as said below
Outputs:
- main_tiles: float32 [16, 8, 1024, 1024], P('row', 'col', 'rep')
- half_tiles: float32 [16, 1024, 1024], P('row', 'rep', 'col')
Inputs may be any that keep to these rules, and one draw needn't show every extreme that they name: `genotypes`: imputed dosages of the alternate allele, real-valued.
All inputs are finite; a program needn't handle non-finite values.
Results may differ from a plain program's by a relative error of at most 0.008.
Values may be sent and summed in bfloat16 or wider, within the bound.
No kernel may reach another device: no remote copies, remote signals or barrier semaphores. Data moves between devices by JAX's collectives and lax.ppermute only.
A program may use at most 64 MiB of HBM per device.

v0:
```python
import jax
import jax.numpy as jnp
import numpy as np
from jax import lax
from jax.sharding import PartitionSpec as P


def copy_for_each(x, axis):
    copies = jnp.broadcast_to(x, (lax.axis_size(axis), *x.shape))
    return lax.all_to_all(copies, axis, split_axis=0, concat_axis=0, tiled=True)


def over_copies(x, axis):
    return copy_for_each(x, axis).sum(axis=0)


def packed_total(arrays, axis):
    ends = [0]
    for a in arrays:
        ends.append(ends[-1] + a.size)
    total = over_copies(jnp.concatenate([a.ravel() for a in arrays]), axis)
    return tuple((total[b:e].reshape(a.shape) for a, b, e in zip(arrays, ends, ends[1:])))


def cut_along(x, dim, length):
    before, after = (x.shape[:dim], x.shape[dim + 1 :])
    return jnp.moveaxis(x.reshape(*before, length, -1, *after), dim, 0)


def summed_on_arrival(x, axis, dim):
    length = lax.axis_size(axis)
    blocks = lax.all_to_all(cut_along(x, dim, length), axis, 0, 0, tiled=True)
    return jnp.sum(blocks.astype(jnp.float32), axis=0)


def body(genotypes):
    sample_rows, variants = genotypes.shape
    row_count = lax.axis_size("row")
    col_count = lax.axis_size("col")
    rep_count = lax.axis_size("rep")
    sample_count = sample_rows * row_count * col_count * rep_count
    block_width = variants // row_count
    slab_width = block_width // col_count
    pair_count = row_count * col_count
    blocked = genotypes.reshape(sample_rows, row_count, block_width)
    shift_table = np.array(
        [(brow + bcol) % row_count for brow in range(row_count) for bcol in range(col_count)],
        np.int32,
    )
    partner = jnp.take(blocked, shift_table, axis=1)
    slab_view = genotypes.reshape(sample_rows, pair_count, slab_width)
    far_slab = jnp.roll(slab_view, -(pair_count // 2), axis=1)
    own_block = jnp.broadcast_to(
        blocked[:, :, None, :], (sample_rows, row_count, col_count, block_width)
    )
    payload = jnp.concatenate(
        [partner, own_block.reshape(sample_rows, pair_count, block_width), far_slab], axis=2
    )
    payload_width = payload.shape[2]
    arrived = lax.all_to_all(payload, ("row", "col"), split_axis=1, concat_axis=0, tiled=True)
    arrived = arrived.reshape(-1, payload_width)
    values = arrived.astype(jnp.float32)
    col_dose, col_square = packed_total(
        (jnp.sum(values, axis=0), jnp.sum(values * values, axis=0)), "rep"
    )
    col_mean = col_dose / sample_count
    col_spread = col_square / sample_count - col_mean * col_mean
    arrived = ((values - col_mean) * lax.rsqrt(col_spread + 1e-05)).astype(jnp.bfloat16)
    scale_factor = 1.0 / sample_count
    right_side = jnp.concatenate(
        [arrived[:, :block_width], arrived[:, payload_width - slab_width :]], axis=1
    )
    product = lax.dot_general(
        arrived[:, block_width : 2 * block_width],
        right_side,
        (((0,), (0,)), ((), ())),
        preferred_element_type=jnp.float32,
    )
    partial_value = product * scale_factor
    summed = summed_on_arrival(partial_value.astype(jnp.bfloat16), "rep", 0)
    main_tile = summed[:, :block_width].reshape(1, 1, -1, block_width)
    half_tile = summed[:, block_width:].reshape(1, -1, slab_width)
    return (main_tile, half_tile)


def solution(mesh):
    placed = (P(("row", "col", "rep"), None),)
    return jax.shard_map(
        body,
        mesh=mesh,
        in_specs=placed,
        out_specs=(P("row", "col", "rep", None), P("row", "rep", "col")),
        check_vma=False,
    )
```

profile of v0, /device:TPU:9, one launch (start us, length us, event | category | flops | bytes accessed | tf_op | source)
XLA Modules:
  0.0 138.4 jit_solution(16736934565368421999)
XLA Ops:
  0.6 0.0 copy-start
  0.6 0.7 pad_clamp_fusion
  1.3 0.9 fusion.10
  2.3 2.4 %gather_fusion = bf16[128,4,1024]{2,1,0:T(4,128)(2,1)S(1)} fusion(bf16[4,16,1024]{2,0,1:T(4,128)(2,1)} %bitcast.16, s32[1024]{0:T(1024)S(1)} %pad_clamp_fusion), kind=kCustom, calls=%fused_computation | custom fusion | bytes 2097664 | tf_op jit(solution)/shard_map/jit(_take)/gather | solution.py:50
  4.6 0.0 copy-done
  4.6 0.3 broadcast_in_dim.25
  4.9 5.4 %maximum_maximum_fusion = bf16[4,128,2176]{2,0,1:T(4,128)(2,1)S(1)} fusion(bf16[4,64,128]{2,0,1:T(4,128)(2,1)S(1)} %get-tuple-element.5, bf16[4,64,128]{2,0,1:T(4,128)(2,1)S(1)} %get-tuple-element.4, bf16[4,128,1024]{2,0,1:T(4,128)(2,1)S(1)} %bitcast.19, bf16[4,128,1024]{2,0,1:T(4,128)(2,1)S(1)} %bitcast.18), kind=kLoop, calls=%fused_computation.9 | loop fusion | flops 8912896 | bytes 4456448 | tf_op jit(solution)/shard_map/concatenate | solution.py:56
  10.4 73.1 %all_to_all.20 = bf16[4,128,2176]{2,0,1:T(4,128)(2,1)S(1)} all-to-all(bf16[4,128,2176]{2,0,1:T(4,128)(2,1)S(1)} %maximum_maximum_fusion), channel_id=1, replica_groups=mesh['row'=16,'col'=8,'rep'=4] {'row','col'}, dimensions={1} | all-to-all | bytes 4456448 | tf_op jit(solution)/shard_map/all_to_all | solution.py:60
  83.5 1.8 %convert_reduce_fusion = (f32[2176]{0:T(1024)S(1)}, f32[2176]{0:T(1024)S(1)}) fusion(bf16[4,128,2176]{2,0,1:T(4,128)(2,1)S(1)} %all_to_all.20), kind=kLoop, calls=%fused_computation.2 | loop fusion | flops 4452096 | bytes 2245632 | tf_op jit(solution)/shard_map/reduce_sum | solution.py:64
  85.3 0.7 broadcast_in_dim.26
  85.9 4.0 %all-to-all-start.1 = ((f32[4,1,4352]{2,1,0:T(1,128)}), f32[4,1,4352]{2,1,0:T(1,128)S(1)}, u32[]{:S(2)}, u32[]{:S(2)}) async-start(f32[4,1,4352]{2,1,0:T(1,128)} %broadcast_in_dim.26), calls=%async_computation.1 | async-start | bytes 139264 | tf_op jit(solution)/shard_map/all_to_all | solution.py:10
  89.9 2.6 %convert_bitcast_fusion = f32[128,4,1,2176]{3,1,0,2:T(4,128)} fusion(bf16[4,128,2176]{2,0,1:T(4,128)(2,1)S(1)} %all_to_all.20), kind=kLoop, calls=%fused_computation.3 | loop fusion | flops 1114112 | bytes 6684672 | tf_op jit(solution)/shard_map/convert_element_type | solution.py:62
  92.5 5.6 %reshape.48 = f32[512,2176]{1,0:T(8,128)} reshape(f32[128,4,1,2176]{3,1,0,2:T(4,128)} %convert_bitcast_fusion) | data formatting | bytes 8912896 | tf_op jit(solution)/shard_map/convert_element_type | solution.py:62
  98.1 0.0 all-to-all-done.1
  98.1 0.1 reduce_sum.38
  98.2 2.7 %multiply_convert_fusion = bf16[512,2176]{1,0:T(8,128)(2,1)S(1)} fusion(f32[512,2176]{1,0:T(8,128)} %reshape.48, f32[2176]{0:T(1024)S(1)} %get-tuple-element.7, f32[2176]{0:T(1024)S(1)} %get-tuple-element.6), kind=kLoop, calls=%fused_computation.7 | loop fusion | flops 3342336 | bytes 6702080 | tf_op jit(solution)/shard_map/convert_element_type | solution.py:68
  100.9 0.1 slice.45
  101.0 1.6 %fusion.1 = bf16[1024,1152]{1,0:T(8,128)(2,1)S(1)} fusion(bf16[512,128]{1,0:T(8,128)(2,1)S(1)} %slice.46, bf16[512,1024]{1,0:T(8,128)(2,1)S(1)} %slice.45, bf16[512,2176]{1,0:T(8,128)(2,1)S(1)} %multiply_convert_fusion), kind=kOutput, calls=%fused_computation.8 | convolution fusion | flops 1212678144 | bytes 4587520 | tf_op jit(solution)/shard_map/dot_general | solution.py:73
  102.6 33.7 %all_to_all.21 = bf16[4,256,1152]{2,1,0:T(8,128)(2,1)S(1)} all-to-all(bf16[4,256,1152]{2,1,0:T(8,128)(2,1)S(1)} %bitcast.20), channel_id=1, replica_groups=mesh['row'=16,'col'=8,'rep'=4] {'rep'}, dimensions={0} | all-to-all | bytes 4718592 | tf_op jit(solution)/shard_map/all_to_all | solution.py:32
  136.3 0.3 convert_reduce_fusion.1
  136.6 0.7 slice_bitcast_fusion.1
  137.3 1.1 slice_bitcast_fusion
  (3 shorter events, 0.0 us)
Async XLA Ops:
  0.6 4.0 %copy-start = (bf16[4,16384]{1,0:T(4,128)(2,1)S(1)}, bf16[4,16384]{1,0:T(4,128)(2,1)}, u32[]{:S(2)}) copy-start(bf16[4,16384]{1,0:T(4,128)(2,1)} %param.2) | copy-start | bytes 393220
  85.9 12.2 %all-to-all-start.1 = ((f32[4,1,4352]{2,1,0:T(1,128)}), f32[4,1,4352]{2,1,0:T(1,128)S(1)}, u32[]{:S(2)}, u32[]{:S(2)}) async-start(f32[4,1,4352]{2,1,0:T(1,128)} %broadcast_in_dim.26), calls=%async_computation.1 | async-start | bytes 139264 | tf_op jit(solution)/shard_map/all_to_all | solution.py:10
where the time goes:
time: 139 us; the launch traced here: 138 us
  blocking collectives  107 us (77%)
  other arithmetic  13.6 us (10%)
  local copies, waits for them, and re-layouts  11.7 us (8%)
  starting transfers between devices  4.01 us (3%)
  matrix products  1.59 us (1%)
    all_to_all x1, blocking collectives, body(): lax.all_to_all(payload, ('row', 'col'), split_axis=1, concat_axis=0, tile...  73.1 us
    all_to_all x1, blocking collectives, summed_on_arrival(): blocks = lax.all_to_all(cut_along(x, dim, length), axis, 0, 0, tiled=True)  33.7 us
    convert_element_type x1, local copies, waits for them, and re-layouts, body(): values = arrived.astype(jnp.float32)  5.55 us
    concatenate x1, other arithmetic, body(): jnp.concatenate([partner, own_block.reshape(sample_rows, pair_count, bloc...  5.44 us
    all_to_all x1, starting transfers between devices, copy_for_each(): return lax.all_to_all(copies, axis, split_axis=0, concat_axis=0, tiled=True)  4.01 us
  transfers between devices with their start and end apart: 1, of which 0 were waited for; matrix products, arithmetic and copies ran while one was open for 6% of the time, Pallas kernels for 0%

commit v1 on v0

--- a/solution.py
+++ b/solution.py
@@ -57,7 +57,15 @@
         [partner, own_block.reshape(sample_rows, pair_count, block_width), far_slab], axis=2
     )
     payload_width = payload.shape[2]
-    arrived = lax.all_to_all(payload, ("row", "col"), split_axis=1, concat_axis=0, tiled=True)
+    arrived = jnp.concatenate(
+        lax.all_to_all(
+            jnp.stack(jnp.split(payload, lax.axis_size(("row", "col")), axis=1)),
+            ("row", "col"),
+            0,
+            0,
+        ),
+        axis=0,
+    )
     arrived = arrived.reshape(-1, payload_width)
     values = arrived.astype(jnp.float32)
     col_dose, col_square = packed_total(

time: 139 us -> 136 us (0.978)
  other arithmetic: 13.6 us -> 11 us
  blocking collectives: 107 us -> 105 us
  waiting for transfers between devices: 0.01 us -> 1.94 us
    convert_element_type x1, local copies, waits for them, and re-layouts: 5.55 us -> 2.55 us  [body(): values = arrived.astype(jnp.float32)]
    convert_element_type x1 -> x0, other arithmetic: 2.61 us -> none  [body(): values = arrived.astype(jnp.float32)]
    all_to_all x1, blocking collectives: 33.7 us -> 31.5 us  [summed_on_arrival(): blocks = lax.all_to_all(cut_along(x, dim, length), axis, 0, 0, tiled=True)]
    unnamed x2 -> x129, local copies, waits for them, and re-layouts: 0.01 us -> 2.14 us
    all_to_all x1, waiting for transfers between devices: 0.01 us -> 1.94 us  [copy_for_each(): return lax.all_to_all(copies, axis, split_axis=0, concat_axis=0, tiled=True)]
  transfers between devices with their start and end apart: 1 -> 1, of which waited for: 0 -> 1; matrix products, arithmetic and copies ran while one was open for 6% -> 2% of each run, Pallas kernels for 0% -> 0%
where the time goes in v1:
time: 136 us; the launch traced here: 135 us
  blocking collectives  105 us (77%)
  other arithmetic  11 us (8%)
  local copies, waits for them, and re-layouts  10.9 us (8%)
  starting transfers between devices  4.01 us (3%)
  waiting for transfers between devices  1.94 us (1%)
  matrix products  1.59 us (1%)
    all_to_all x1, blocking collectives, body(): lax.all_to_all(jnp.stack(jnp.split(payload, lax.axis_size(('row', 'col'))...  73.1 us
    all_to_all x1, blocking collectives, summed_on_arrival(): blocks = lax.all_to_all(cut_along(x, dim, length), axis, 0, 0, tiled=True)  31.5 us
    concatenate x1, other arithmetic, body(): jnp.concatenate([partner, own_block.reshape(sample_rows, pair_count, bloc...  5.44 us
    all_to_all x1, starting transfers between devices, copy_for_each(): return lax.all_to_all(copies, axis, split_axis=0, concat_axis=0, tiled=True)  4.01 us
  transfers between devices with their start and end apart: 1, of which 1 were waited for; matrix products, arithmetic and copies ran while one was open for 2% of the time, Pallas kernels for 0%

profile of v1, /device:TPU:9, one launch (start us, length us, event | category | flops | bytes accessed | tf_op | source)
XLA Modules:
  0.0 135.3 jit_solution(6326807295650649874)
XLA Ops:
  0.6 0.0 copy-start
  0.6 0.7 pad_clamp_fusion
  1.3 0.9 fusion.9
  2.3 2.4 %gather_fusion = bf16[128,4,1024]{2,1,0:T(4,128)(2,1)S(1)} fusion(bf16[4,16,1024]{2,0,1:T(4,128)(2,1)} %bitcast.524, s32[1024]{0:T(1024)S(1)} %pad_clamp_fusion), kind=kCustom, calls=%fused_computation | custom fusion | bytes 2097664 | tf_op jit(solution)/shard_map/jit(_take)/gather | solution.py:50
  4.6 0.0 copy-done
  4.6 0.3 broadcast_in_dim.25
  4.9 5.4 %maximum_maximum_fusion = bf16[4,128,2176]{2,0,1:T(4,128)(2,1)S(1)} fusion(bf16[4,64,128]{2,0,1:T(4,128)(2,1)S(1)} %get-tuple-element.5, bf16[4,64,128]{2,0,1:T(4,128)(2,1)S(1)} %get-tuple-element.4, bf16[4,128,1024]{2,0,1:T(4,128)(2,1)S(1)} %bitcast.527, bf16[4,128,1024]{2,0,1:T(4,128)(2,1)S(1)} %bitcast.526), kind=kLoop, calls=%fused_computation.6 | loop fusion | flops 8912896 | bytes 4456448 | tf_op jit(solution)/shard_map/concatenate | solution.py:56
  13.2 73.1 %all_to_all.16 = bf16[128,4,1,2176]{3,1,2,0:T(4,128)(2,1)S(1)} all-to-all(bf16[128,4,1,2176]{3,1,2,0:T(4,128)(2,1)S(1)} %constant_dynamic-update-slice_fusion), channel_id=1, replica_groups=mesh['row'=16,'col'=8,'rep'=4] {'row','col'}, dimensions={0} | all-to-all | bytes 4456448 | tf_op jit(solution)/shard_map/all_to_all | solution.py:61
  86.2 1.8 %convert_reduce_fusion.1 = (f32[2176]{0:T(1024)S(1)}, f32[2176]{0:T(1024)S(1)}) fusion(bf16[128,4,1,2176]{3,1,2,0:T(4,128)(2,1)S(1)} %all_to_all.16), kind=kLoop, calls=%fused_computation.7 | loop fusion | flops 4452096 | bytes 2245632 | tf_op jit(solution)/shard_map/reduce_sum | solution.py:72
  88.0 0.7 broadcast_in_dim.26
  88.7 4.0 %all-to-all-start.1 = ((f32[4,1,4352]{2,1,0:T(1,128)}), f32[4,1,4352]{2,1,0:T(1,128)S(1)}, u32[]{:S(2)}, u32[]{:S(2)}) async-start(f32[4,1,4352]{2,1,0:T(1,128)} %broadcast_in_dim.26), calls=%async_computation.1 | async-start | bytes 139264 | tf_op jit(solution)/shard_map/all_to_all | solution.py:10
  92.7 2.6 %reshape.42 = f32[512,2176]{1,0:T(8,128)} reshape(bf16[128,4,1,2176]{3,1,2,0:T(4,128)(2,1)S(1)} %all_to_all.16) | data formatting | bytes 6684672 | tf_op jit(solution)/shard_map/convert_element_type | solution.py:70
  95.3 1.9 %all-to-all-done.1 = f32[4,1,4352]{2,1,0:T(1,128)S(1)} async-done(((f32[4,1,4352]{2,1,0:T(1,128)}), f32[4,1,4352]{2,1,0:T(1,128)S(1)}, u32[]{:S(2)}, u32[]{:S(2)}) %all-to-all-start.1) | async-done | bytes 69664 | tf_op jit(solution)/shard_map/all_to_all | solution.py:10
  97.2 0.1 reduce_sum.38
  97.3 2.7 %multiply_convert_fusion = bf16[512,2176]{1,0:T(8,128)(2,1)S(1)} fusion(f32[512,2176]{1,0:T(8,128)} %reshape.42, f32[2176]{0:T(1024)S(1)} %get-tuple-element.7, f32[2176]{0:T(1024)S(1)} %get-tuple-element.6), kind=kLoop, calls=%fused_computation.3 | loop fusion | flops 3342336 | bytes 6702080 | tf_op jit(solution)/shard_map/convert_element_type | solution.py:76
  100.0 0.1 slice.45
  100.1 1.6 %fusion = bf16[1024,1152]{1,0:T(8,128)(2,1)S(1)} fusion(bf16[512,128]{1,0:T(8,128)(2,1)S(1)} %slice.46, bf16[512,1024]{1,0:T(8,128)(2,1)S(1)} %slice.45, bf16[512,2176]{1,0:T(8,128)(2,1)S(1)} %multiply_convert_fusion), kind=kOutput, calls=%fused_computation.5 | convolution fusion | flops 1212678144 | bytes 4587520 | tf_op jit(solution)/shard_map/dot_general | solution.py:81
  101.7 31.5 %all_to_all.17 = bf16[4,256,1152]{2,1,0:T(8,128)(2,1)S(1)} all-to-all(bf16[4,256,1152]{2,1,0:T(8,128)(2,1)S(1)} %bitcast.528), channel_id=1, replica_groups=mesh['row'=16,'col'=8,'rep'=4] {'rep'}, dimensions={0} | all-to-all | bytes 4718592 | tf_op jit(solution)/shard_map/all_to_all | solution.py:32
  133.2 0.3 convert_reduce_fusion
  133.5 0.7 slice_bitcast_fusion.1
  134.2 1.1 slice_bitcast_fusion
  (131 shorter events, 2.2 us)
Async XLA Ops:
  0.6 4.0 %copy-start = (bf16[4,16384]{1,0:T(4,128)(2,1)S(1)}, bf16[4,16384]{1,0:T(4,128)(2,1)}, u32[]{:S(2)}) copy-start(bf16[4,16384]{1,0:T(4,128)(2,1)} %param.2) | copy-start | bytes 393220
  88.7 8.5 %all-to-all-start.1 = ((f32[4,1,4352]{2,1,0:T(1,128)}), f32[4,1,4352]{2,1,0:T(1,128)S(1)}, u32[]{:S(2)}, u32[]{:S(2)}) async-start(f32[4,1,4352]{2,1,0:T(1,128)} %broadcast_in_dim.26), calls=%async_computation.1 | async-start | bytes 139264 | tf_op jit(solution)/shard_map/all_to_all | solution.py:10
